TPU v7x, 32 devices: a whole 2x2x4 slice. The times are simulated.
32 devices in a mesh: dp: 8 (over z, x), bn: 4 (over y, core).
Axes of the slice: x: 2, y: 2, z: 4, core: 2. Of those that a mesh axis runs over, the one named last changes fastest.
Arguments:
- features: bfloat16 [512, 8, 2048], P(('dp', 'bn')), may hold values from -6 to 6
- shuffle_masks: int32 [16], replicated, may hold values from 0 to 7, as said below
- conv_in: bfloat16 [2048, 512], replicated, may hold values from -0.125 to 0.125
- conv_mid: bfloat16 [3, 512, 512], replicated, may hold values from -0.15625 to 0.15625
- conv_out: bfloat16 [512, 2048], replicated, may hold values from -0.25 to 0.25
- head: bfloat16 [2048, 128], replicated, may hold values from -0.125 to 0.125
- queries: bfloat16 [512, 128], P(('dp', 'bn'))
- queue: bfloat16 [65536, 128], P('dp')
- positive: int32 [512], P(('dp', 'bn')), may hold values from 0 to 511, as said below
Outputs:
- loss_rows: float32 [512], P(('dp', 'bn'))
Inputs may be any that keep to these rules, and one draw needn't show every extreme that they name: `shuffle_masks`: every binary digit of a dp index is set in exactly half of the entries. positive[i] names a crop with the same bn index as crop i.
All inputs are finite; a program needn't handle non-finite values.
Results may differ from a plain program's by a relative error of at most 0.0023.
Values may be sent and summed in bfloat16 or wider, within the bound.
A program may use at most 64 MiB of HBM per device.

v0:
```python
import jax
import jax.numpy as jnp
from jax import lax
from jax.sharding import PartitionSpec as P

EPS_BN = 1e-05
EPS_UNIT = 1e-06
INV_TEMP = 1.0 / 0.07


def partner_2(value, axis, distance):
    return lax.ppermute(value, axis, [(i, i ^ 1 << distance) for i in range(lax.axis_size(axis))])


def unit_rows(values):
    values = values.astype(jnp.float32)
    return values * lax.rsqrt(jnp.sum(values * values, axis=-1, keepdims=True) + EPS_UNIT)


def group_norm(values, row_total):
    first = lax.psum(jnp.sum(values, axis=0), "bn")
    center = first / row_total
    spread = lax.psum(jnp.sum(jnp.square(values - center), axis=0), "bn") / row_total
    return (values - center) * lax.rsqrt(spread + EPS_BN)


def moving_slots(shuffle_masks, level, half):
    flags = jnp.bitwise_and(jnp.right_shift(shuffle_masks, level), 1)
    return jnp.argsort(1 - flags, stable=True)[:half]


def on_device(features, shuffle_masks, conv_in, conv_mid, conv_out, head, queries, queue, positive):
    dp_count = lax.axis_size("dp")
    bn_count = lax.axis_size("bn")
    bit_count = dp_count.bit_length() - 1
    crop_dev, positions, channels = features.shape
    half = crop_dev // 2
    middle = conv_in.shape[1]
    query_unit = unit_rows(queries).astype(jnp.bfloat16)
    query_all = lax.all_gather(query_unit, "dp", axis=0, tiled=True)
    shuffled = features
    for level in range(bit_count):
        moving = moving_slots(shuffle_masks, level, half)
        partner = partner_2(jnp.take(shuffled, moving, axis=0), "dp", level)
        shuffled = shuffled.at[moving].set(partner)
    row_total = crop_dev * positions * bn_count
    flat_rows = shuffled.reshape(crop_dev * positions, channels)
    first_sum = jnp.dot(flat_rows, conv_in, preferred_element_type=jnp.float32)
    first_act = jax.nn.relu(group_norm(first_sum, row_total)).astype(jnp.bfloat16)
    tap_maps = first_act.reshape(crop_dev, positions, middle)
    padded = jnp.pad(tap_maps, ((0, 0), (1, 1), (0, 0)))
    stacked = jnp.concatenate([padded[:, tap : tap + positions, :] for tap in range(3)], axis=2)
    second_sum = jnp.dot(
        stacked.reshape(crop_dev * positions, 3 * middle),
        conv_mid.reshape(3 * middle, middle),
        preferred_element_type=jnp.float32,
    )
    second_act = jax.nn.relu(group_norm(second_sum, row_total)).astype(jnp.bfloat16)
    third_sum = jnp.dot(second_act, conv_out, preferred_element_type=jnp.float32)
    block = jax.nn.relu(group_norm(third_sum, row_total) + flat_rows.astype(jnp.float32)).astype(
        jnp.bfloat16
    )
    pooled = jnp.mean(
        block.reshape(crop_dev, positions, channels).astype(jnp.float32), axis=1
    ).astype(jnp.bfloat16)
    key_unit = unit_rows(jnp.dot(pooled, head, preferred_element_type=jnp.float32)).astype(
        jnp.bfloat16
    )
    for level in range(bit_count):
        moving = moving_slots(shuffle_masks, level, half)
        partner = partner_2(jnp.take(key_unit, moving, axis=0), "dp", level)
        key_unit = key_unit.at[moving].set(partner)
    queue_unit = unit_rows(queue).astype(jnp.bfloat16)
    scores = jnp.dot(query_all, queue_unit.T, preferred_element_type=jnp.float32) * INV_TEMP
    queue_part = jnp.sum(jnp.exp(scores - INV_TEMP), axis=1)
    key_all = lax.all_gather(key_unit, "dp", axis=0, tiled=True)
    slot_of = positive % crop_dev
    column = positive // crop_dev // bn_count
    picked = jnp.take(key_all, column * crop_dev + slot_of, axis=0)
    positive_logit = (
        jnp.sum(query_unit.astype(jnp.float32) * picked.astype(jnp.float32), axis=-1) * INV_TEMP
    )
    negative = lax.psum_scatter(queue_part, "dp", scatter_dimension=0, tiled=True)
    return jnp.log(jnp.exp(positive_logit - INV_TEMP) + negative) + INV_TEMP - positive_logit


def solution(mesh):
    return jax.shard_map(
        on_device,
        mesh=mesh,
        in_specs=(
            P(("dp", "bn"), None, None),
            P(),
            P(),
            P(),
            P(),
            P(),
            P(("dp", "bn"), None),
            P("dp", None),
            P(("dp", "bn")),
        ),
        out_specs=P(("dp", "bn")),
        check_vma=False,
    )
```

profile of v0, /device:TPU:0, one launch (start us, length us, event | category | flops | bytes accessed | tf_op | source)
XLA Modules:
  0.0 185.4 jit_solution(4941348804758811431)
XLA Ops:
  0.0 1.2 copy.17
  1.9 1.2 sort.51
  3.8 3.0 %collective-permute-start = (bf16[8,8,2048]{2,1,0:T(8,128)(2,1)S(1)}, bf16[8,8,2048]{2,1,0:T(8,128)(2,1)S(1)}, u32[]{:S(2)}, u32[]{:S(2)}) collective-permute-start(bf16[8,8,2048]{2,1,0:T(8,128)(2,1)S(1)} %broadcast_select_fusion.2), channel_id=1, source_target_pairs={{0,4},{4,0},{8,12},{12,8},{16,20},{20,16},{24,28},{28,24},{1,5},{5... | collective-permute-start | bytes 786440 | tf_op jit(solution)/shard_map/ppermute | solution.py:12
  6.8 1.2 sort.52
  8.1 1.2 sort.53
  9.3 3.8 %collective-permute-done = bf16[8,8,2048]{2,1,0:T(8,128)(2,1)S(1)} collective-permute-done((bf16[8,8,2048]{2,1,0:T(8,128)(2,1)S(1)}, bf16[8,8,2048]{2,1,0:T(8,128)(2,1)S(1)}, u32[]{:S(2)}, u32[]{:S(2)}) %collective-permute-start) | collective-permute-done | bytes 262176 | tf_op jit(solution)/shard_map/ppermute | solution.py:12
  13.1 0.8 scatter_fusion
  14.5 1.9 %collective-permute-start.1 = (bf16[8,8,2048]{2,1,0:T(8,128)(2,1)S(1)}, bf16[8,8,2048]{2,1,0:T(8,128)(2,1)S(1)}, u32[]{:S(2)}, u32[]{:S(2)}) collective-permute-start(bf16[8,8,2048]{2,1,0:T(8,128)(2,1)S(1)} %broadcast_select_fusion.1), channel_id=1, source_target_pairs={{0,8},{4,12},{8,0},{12,4},{16,24},{20,28},{24,16},{28,20},{1,9},{5... | collective-permute-start | bytes 786440 | tf_op jit(solution)/shard_map/ppermute | solution.py:12
  16.4 2.7 %fusion.2 = f32[8192]{0:T(1024)S(1)} fusion(bf16[8192,128]{1,0:T(8,128)(2,1)} %param.20), kind=kLoop, calls=%fused_computation.18 | loop fusion | flops 3137536 | bytes 2129920 | tf_op jit(solution)/shard_map/reduce_sum | solution.py:17
  19.2 2.9 %collective-permute-done.1 = bf16[8,8,2048]{2,1,0:T(8,128)(2,1)S(1)} collective-permute-done((bf16[8,8,2048]{2,1,0:T(8,128)(2,1)S(1)}, bf16[8,8,2048]{2,1,0:T(8,128)(2,1)S(1)}, u32[]{:S(2)}, u32[]{:S(2)}) %collective-permute-start.1) | collective-permute-done | bytes 262176 | tf_op jit(solution)/shard_map/ppermute | solution.py:12
  22.1 0.8 scatter_fusion.1
  23.5 2.6 %collective-permute-start.2 = (bf16[8,8,2048]{2,1,0:T(8,128)(2,1)S(1)}, bf16[8,8,2048]{2,1,0:T(8,128)(2,1)S(1)}, u32[]{:S(2)}, u32[]{:S(2)}) collective-permute-start(bf16[8,8,2048]{2,1,0:T(8,128)(2,1)S(1)} %broadcast_select_fusion), channel_id=1, source_target_pairs={{0,16},{4,20},{8,24},{12,28},{16,0},{20,4},{24,8},{28,12},{1,17},{... | collective-permute-start | bytes 786440 | tf_op jit(solution)/shard_map/ppermute | solution.py:12
  26.2 10.5 %collective-permute-done.2 = bf16[8,8,2048]{2,1,0:T(8,128)(2,1)S(1)} collective-permute-done((bf16[8,8,2048]{2,1,0:T(8,128)(2,1)S(1)}, bf16[8,8,2048]{2,1,0:T(8,128)(2,1)S(1)}, u32[]{:S(2)}, u32[]{:S(2)}) %collective-permute-start.2) | collective-permute-done | bytes 262176 | tf_op jit(solution)/shard_map/ppermute | solution.py:12
  37.4 2.1 %fusion.34 = (f32[512]{0:T(512)S(1)}, f32[128,512]{1,0:T(8,128)S(1)}) fusion(bf16[2048,512]{1,0:T(8,128)(2,1)} %param.15, bf16[16,8,2048]{2,1,0:T(8,128)(2,1)S(1)} %scatter_fusion.2), kind=kOutput, calls=%fused_computation.102 | convolution fusion | flops 268500480 | bytes 2885632 | tf_op jit(solution)/shard_map/dot_general | solution.py:48
  39.5 5.7 %psum.42 = f32[512]{0:T(512)S(1)} all-reduce(f32[512]{0:T(512)S(1)} %get-tuple-element.28), channel_id=1, replica_groups=mesh['dp'=8,'bn'=4] {'bn'}, use_global_device_ids=true, to_apply=%region_8.10 | all-reduce | flops 512 | bytes 4096 | tf_op jit(solution)/shard_map/psum | solution.py:21
  45.2 6.5 %psum.43 = f32[512]{0:T(512)S(1)} all-reduce(f32[512]{0:T(512)S(1)} %multiply_reduce_fusion.2), channel_id=1, replica_groups=mesh['dp'=8,'bn'=4] {'bn'}, use_global_device_ids=true, to_apply=%region_10.12 | all-reduce | flops 512 | bytes 4096 | tf_op jit(solution)/shard_map/psum | solution.py:23
  51.9 1.8 fusion.35
  53.7 5.7 %psum.44 = f32[512]{0:T(512)S(1)} all-reduce(f32[512]{0:T(512)S(1)} %get-tuple-element.30), channel_id=1, replica_groups=mesh['dp'=8,'bn'=4] {'bn'}, use_global_device_ids=true, to_apply=%region_12.14 | all-reduce | flops 512 | bytes 4096 | tf_op jit(solution)/shard_map/psum | solution.py:21
  59.5 6.2 %psum.45 = f32[512]{0:T(512)S(1)} all-reduce(f32[512]{0:T(512)S(1)} %multiply_reduce_fusion.1), channel_id=1, replica_groups=mesh['dp'=8,'bn'=4] {'bn'}, use_global_device_ids=true, to_apply=%region_14.16 | all-reduce | flops 512 | bytes 4096 | tf_op jit(solution)/shard_map/psum | solution.py:23
  65.7 1.4 fusion.36
  67.2 5.9 %psum.46 = f32[2048]{0:T(1024)S(1)} all-reduce(f32[2048]{0:T(1024)S(1)} %get-tuple-element.32), channel_id=1, replica_groups=mesh['dp'=8,'bn'=4] {'bn'}, use_global_device_ids=true, to_apply=%region_16.18 | all-reduce | flops 2048 | bytes 16384 | tf_op jit(solution)/shard_map/psum | solution.py:21
  73.1 1.3 multiply_reduce_fusion
  74.4 6.7 %psum.47 = f32[2048]{0:T(1024)S(1)} all-reduce(f32[2048]{0:T(1024)S(1)} %multiply_reduce_fusion), channel_id=1, replica_groups=mesh['dp'=8,'bn'=4] {'bn'}, use_global_device_ids=true, to_apply=%region_18.20 | all-reduce | flops 2048 | bytes 16384 | tf_op jit(solution)/shard_map/psum | solution.py:23
  81.2 1.7 convert_reduce_fusion
  84.7 2.9 %collective-permute-done.3 = bf16[8,128]{1,0:T(8,128)(2,1)S(1)} collective-permute-done((bf16[8,128]{1,0:T(8,128)(2,1)S(1)}, bf16[8,128]{1,0:T(8,128)(2,1)S(1)}, u32[]{:S(2)}, u32[]{:S(2)}) %collective-permute-start.3) | collective-permute-done | bytes 2080 | tf_op jit(solution)/shard_map/ppermute | solution.py:12
  89.0 3.3 %collective-permute-done.4 = bf16[8,128]{1,0:T(8,128)(2,1)S(1)} collective-permute-done((bf16[8,128]{1,0:T(8,128)(2,1)S(1)}, bf16[8,128]{1,0:T(8,128)(2,1)S(1)}, u32[]{:S(2)}, u32[]{:S(2)}) %collective-permute-start.4) | collective-permute-done | bytes 2080 | tf_op jit(solution)/shard_map/ppermute | solution.py:12
  93.6 1.6 collective-permute-start.5
  96.5 1.6 collective-permute-done.5
  98.7 30.4 %all_gather.6 = bf16[128,128]{1,0:T(8,128)(2,1)S(1)} all-gather(bf16[16,128]{1,0:T(8,128)(2,1)S(1)} %scatter_fusion.5), channel_id=1, replica_groups=mesh['dp'=8,'bn'=4] {'dp'}, dimensions={0}, use_global_device_ids=true | all-gather | bytes 36864 | tf_op jit(solution)/shard_map/all_gather | solution.py:76
  129.9 30.4 %all_gather.7 = bf16[128,128]{1,0:T(8,128)(2,1)S(1)} all-gather(bf16[16,128]{1,0:T(8,128)(2,1)S(1)} %get-tuple-element.14), channel_id=1, replica_groups=mesh['dp'=8,'bn'=4] {'dp'}, dimensions={0}, use_global_device_ids=true | all-gather | bytes 36864 | tf_op jit(solution)/shard_map/all_gather | solution.py:40
  160.3 3.4 %fusion.6 = f32[128]{0:T(128)S(1)} fusion(bf16[128,128]{1,0:T(8,128)(2,1)S(1)} %all_gather.7, bf16[8192,128]{1,0:T(8,128)(2,1)} %param.20, f32[8192]{0:T(1024)S(1)} %add_rsqrt_fusion), kind=kOutput, calls=%fused_computation.21 | convolution fusion | flops 274726784 | bytes 2163200 | tf_op jit(solution)/shard_map/dot_general | solution.py:74
  163.7 21.1 %all-reduce.1 = f32[128]{0:T(128)S(1)} all-reduce(f32[128]{0:T(128)S(1)} %fusion.6), channel_id=2, replica_groups=mesh['dp'=8,'bn'=4] {'dp'}, use_global_device_ids=true, to_apply=%region_27.30.clone | all-reduce | flops 128 | bytes 1024
  (61 shorter events, 10.8 us)
Async XLA Ops:
  0.0 65.7 %copy-start = (bf16[512,2048]{1,0:T(8,128)(2,1)S(1)}, bf16[512,2048]{1,0:T(8,128)(2,1)}, u32[]{:S(2)}) copy-start(bf16[512,2048]{1,0:T(8,128)(2,1)} %param.17) | copy-start | bytes 6291460
  3.8 9.3 %collective-permute-start = (bf16[8,8,2048]{2,1,0:T(8,128)(2,1)S(1)}, bf16[8,8,2048]{2,1,0:T(8,128)(2,1)S(1)}, u32[]{:S(2)}, u32[]{:S(2)}) collective-permute-start(bf16[8,8,2048]{2,1,0:T(8,128)(2,1)S(1)} %broadcast_select_fusion.2), channel_id=1, source_target_pairs={{0,4},{4,0},{8,12},{12,8},{16,20},{20,16},{24,28},{28,24},{1,5},{5... | collective-permute-start | bytes 786440 | tf_op jit(solution)/shard_map/ppermute | solution.py:12
  14.5 11.6 %copy-start.3 = (s32[16]{0:T(128)S(1)}, s32[16]{0:T(128)}, u32[]{:S(2)}) copy-start(s32[16]{0:T(128)} %param.21) | copy-start | bytes 196
  14.5 7.6 %collective-permute-start.1 = (bf16[8,8,2048]{2,1,0:T(8,128)(2,1)S(1)}, bf16[8,8,2048]{2,1,0:T(8,128)(2,1)S(1)}, u32[]{:S(2)}, u32[]{:S(2)}) collective-permute-start(bf16[8,8,2048]{2,1,0:T(8,128)(2,1)S(1)} %broadcast_select_fusion.1), channel_id=1, source_target_pairs={{0,8},{4,12},{8,0},{12,4},{16,24},{20,28},{24,16},{28,20},{1,9},{5... | collective-permute-start | bytes 786440 | tf_op jit(solution)/shard_map/ppermute | solution.py:12
  23.5 13.2 %collective-permute-start.2 = (bf16[8,8,2048]{2,1,0:T(8,128)(2,1)S(1)}, bf16[8,8,2048]{2,1,0:T(8,128)(2,1)S(1)}, u32[]{:S(2)}, u32[]{:S(2)}) collective-permute-start(bf16[8,8,2048]{2,1,0:T(8,128)(2,1)S(1)} %broadcast_select_fusion), channel_id=1, source_target_pairs={{0,16},{4,20},{8,24},{12,28},{16,0},{20,4},{24,8},{28,12},{1,17},{... | collective-permute-start | bytes 786440 | tf_op jit(solution)/shard_map/ppermute | solution.py:12
  67.2 15.7 %copy-start.1 = (bf16[2048,128]{1,0:T(8,128)(2,1)S(1)}, bf16[2048,128]{1,0:T(8,128)(2,1)}, u32[]{:S(2)}) copy-start(bf16[2048,128]{1,0:T(8,128)(2,1)} %param.18) | copy-start | bytes 1572868
  67.2 17.4 %copy-start.2 = (bf16[16,128]{1,0:T(8,128)(2,1)S(1)}, bf16[16,128]{1,0:T(8,128)(2,1)}, u32[]{:S(2)}) copy-start(bf16[16,128]{1,0:T(8,128)(2,1)} %param.19) | copy-start | bytes 12292
  67.2 28.1 %copy-start.4 = (u32[32]{0:T(128)S(1)}, u32[32]{0:T(128)}, u32[]{:S(2)}) copy-start(u32[32]{0:T(128)} %constant.121) | copy-start | bytes 388
  83.9 3.6 %collective-permute-start.3 = (bf16[8,128]{1,0:T(8,128)(2,1)S(1)}, bf16[8,128]{1,0:T(8,128)(2,1)S(1)}, u32[]{:S(2)}, u32[]{:S(2)}) collective-permute-start(bf16[8,128]{1,0:T(8,128)(2,1)S(1)} %broadcast_select_fusion.5), channel_id=1, source_target_pairs={{0,4},{4,0},{8,12},{12,8},{16,20},{20,16},{24,28},{28,24},{1,5},{5... | collective-permute-start | bytes 6152 | tf_op jit(solution)/shard_map/ppermute | solution.py:12
  88.8 3.6 %collective-permute-start.4 = (bf16[8,128]{1,0:T(8,128)(2,1)S(1)}, bf16[8,128]{1,0:T(8,128)(2,1)S(1)}, u32[]{:S(2)}, u32[]{:S(2)}) collective-permute-start(bf16[8,128]{1,0:T(8,128)(2,1)S(1)} %broadcast_select_fusion.4), channel_id=1, source_target_pairs={{0,8},{4,12},{8,0},{12,4},{16,24},{20,28},{24,16},{28,20},{1,9},{5... | collective-permute-start | bytes 6152 | tf_op jit(solution)/shard_map/ppermute | solution.py:12
  93.6 4.5 %collective-permute-start.5 = (bf16[8,128]{1,0:T(8,128)(2,1)S(1)}, bf16[8,128]{1,0:T(8,128)(2,1)S(1)}, u32[]{:S(2)}, u32[]{:S(2)}) collective-permute-start(bf16[8,128]{1,0:T(8,128)(2,1)S(1)} %broadcast_select_fusion.3), channel_id=1, source_target_pairs={{0,16},{4,20},{8,24},{12,28},{16,0},{20,4},{24,8},{28,12},{1,17},{... | collective-permute-start | bytes 6152 | tf_op jit(solution)/shard_map/ppermute | solution.py:12
where the time goes:
time: 186 us; the launch traced here: 185 us
  blocking collectives  119 us (64%)
  waiting for transfers between devices  25 us (13%)
  other arithmetic  12 us (6%)
  starting transfers between devices  9.94 us (5%)
  local copies, waits for them, and re-layouts  9.89 us (5%)
  matrix products  8.99 us (5%)
    all_gather x1, blocking collectives, on_device(): key_all = lax.all_gather(key_unit, 'dp', axis=0, tiled=True)  30.4 us
    all_gather x1, blocking collectives, on_device(): query_all = lax.all_gather(query_unit, 'dp', axis=0, tiled=True)  30.4 us
    ppermute x6, waiting for transfers between devices, partner_2(): lax.ppermute(value, axis, [(i, i ^ 1 << distance) for i in range(lax.axis...  25 us
    unnamed x1, blocking collectives  21.1 us
    psum x3, blocking collectives, group_norm(): lax.psum(jnp.sum(jnp.square(values - center), axis=0), 'bn') / row_total  19.5 us
    psum x3, blocking collectives, group_norm(): first = lax.psum(jnp.sum(values, axis=0), 'bn')  17.2 us
    ppermute x6, starting transfers between devices, partner_2(): lax.ppermute(value, axis, [(i, i ^ 1 << distance) for i in range(lax.axis...  9.94 us
    sort x3, other arithmetic, moving_slots(): return jnp.argsort(1 - flags, stable=True)[:half]  3.74 us
  transfers between devices with their start and end apart: 6, of which 6 were waited for; matrix products, arithmetic and copies ran while one was open for 3% of the time, Pallas kernels for 0%

commit v1 on v0

--- a/solution.py
+++ b/solution.py
@@ -6,6 +6,26 @@
 EPS_BN = 1e-05
 EPS_UNIT = 1e-06
 INV_TEMP = 1.0 / 0.07
+
+
+def do_the_scenes(target, in_dim):
+    target = jnp.moveaxis(target, 0, in_dim)
+    t1 = target.shape
+    t_next = target.reshape(*t1[:in_dim], t1[in_dim] * t1[in_dim + 1], *t1[in_dim + 2 :])
+    return t_next
+
+
+def apply_outputs(load, mesh_ax):
+    opened = lax.psum(1, mesh_ax)
+    seen_now = lax.axis_index(mesh_ax)
+    outer, block_last = (opened, seen_now)
+    w1, low = (load[None], 1)
+    while low < outer:
+        w2 = lax.ppermute(w1, mesh_ax, [(q, q ^ low) for q in range(outer)])
+        y = block_last & low == 0
+        w1 = jnp.concatenate([jnp.where(y, w1, w2), jnp.where(y, w2, w1)])
+        low *= 2
+    return w1
 
 
 def partner_2(value, axis, distance):
@@ -73,7 +93,7 @@
     queue_unit = unit_rows(queue).astype(jnp.bfloat16)
     scores = jnp.dot(query_all, queue_unit.T, preferred_element_type=jnp.float32) * INV_TEMP
     queue_part = jnp.sum(jnp.exp(scores - INV_TEMP), axis=1)
-    key_all = lax.all_gather(key_unit, "dp", axis=0, tiled=True)
+    key_all = do_the_scenes(apply_outputs(key_unit, "dp"), 0)
     slot_of = positive % crop_dev
     column = positive // crop_dev // bn_count
     picked = jnp.take(key_all, column * crop_dev + slot_of, axis=0)

time: 186 us -> 168 us (0.903)
  blocking collectives: 119 us -> 88.2 us
  starting transfers between devices: 9.94 us -> 16.3 us
  waiting for transfers between devices: 25 us -> 30.7 us
    all_gather x1 -> x0, blocking collectives: 30.4 us -> none  [on_device(): key_all = lax.all_gather(key_unit, 'dp', axis=0, tiled=True)]
    ppermute x0 -> x3, waiting for transfers between devices: none -> 5.68 us  [apply_outputs(): w2 = lax.ppermute(w1, mesh_ax, [(q, q ^ low) for q in range(outer)])]
    ppermute x0 -> x3, starting transfers between devices: none -> 5.04 us  [apply_outputs(): w2 = lax.ppermute(w1, mesh_ax, [(q, q ^ low) for q in range(outer)])]
  transfers between devices with their start and end apart: 6 -> 9, of which waited for: 6 -> 9; matrix products, arithmetic and copies ran while one was open for 3% -> 4% of each run, Pallas kernels for 0% -> 0%
where the time goes in v1:
time: 168 us; the launch traced here: 167 us
  blocking collectives  88.2 us (52%)
  waiting for transfers between devices  30.7 us (18%)
  starting transfers between devices  16.3 us (10%)
  other arithmetic  12 us (7%)
  local copies, waits for them, and re-layouts  9.9 us (6%)
  matrix products  8.97 us (5%)
    all_gather x1, blocking collectives, on_device(): query_all = lax.all_gather(query_unit, 'dp', axis=0, tiled=True)  30.9 us
    ppermute x6, waiting for transfers between devices, partner_2(): lax.ppermute(value, axis, [(i, i ^ 1 << distance) for i in range(lax.axis...  25.1 us
    unnamed x1, blocking collectives  20.6 us
    psum x3, blocking collectives, group_norm(): lax.psum(jnp.sum(jnp.square(values - center), axis=0), 'bn') / row_total  19.5 us
    psum x3, blocking collectives, group_norm(): first = lax.psum(jnp.sum(values, axis=0), 'bn')  17.2 us
    ppermute x6, starting transfers between devices, partner_2(): lax.ppermute(value, axis, [(i, i ^ 1 << distance) for i in range(lax.axis...  11.3 us
    ppermute x3, waiting for transfers between devices, apply_outputs(): w2 = lax.ppermute(w1, mesh_ax, [(q, q ^ low) for q in range(outer)])  5.68 us
    ppermute x3, starting transfers between devices, apply_outputs(): w2 = lax.ppermute(w1, mesh_ax, [(q, q ^ low) for q in range(outer)])  5.04 us
  transfers between devices with their start and end apart: 9, of which 9 were waited for; matrix products, arithmetic and copies ran while one was open for 4% of the time, Pallas kernels for 0%

profile of v1, /device:TPU:0, one launch (start us, length us, event | category | flops | bytes accessed | tf_op | source)
XLA Modules:
  0.0 167.1 jit_solution(8252388892318094309)
XLA Ops:
  1.9 1.2 sort.51
  3.8 3.0 %collective-permute-start = (bf16[8,8,2048]{2,1,0:T(8,128)(2,1)S(1)}, bf16[8,8,2048]{2,1,0:T(8,128)(2,1)S(1)}, u32[]{:S(2)}, u32[]{:S(2)}) collective-permute-start(bf16[8,8,2048]{2,1,0:T(8,128)(2,1)S(1)} %broadcast_select_fusion.2), channel_id=1, source_target_pairs={{0,4},{4,0},{8,12},{12,8},{16,20},{20,16},{24,28},{28,24},{1,5},{5... | collective-permute-start | bytes 786440 | tf_op jit(solution)/shard_map/ppermute | solution.py:32
  6.8 1.2 sort.52
  8.0 1.2 sort.53
  9.3 3.8 %collective-permute-done = bf16[8,8,2048]{2,1,0:T(8,128)(2,1)S(1)} collective-permute-done((bf16[8,8,2048]{2,1,0:T(8,128)(2,1)S(1)}, bf16[8,8,2048]{2,1,0:T(8,128)(2,1)S(1)}, u32[]{:S(2)}, u32[]{:S(2)}) %collective-permute-start) | collective-permute-done | bytes 262176 | tf_op jit(solution)/shard_map/ppermute | solution.py:32
  14.5 1.9 %collective-permute-start.1 = (bf16[8,8,2048]{2,1,0:T(8,128)(2,1)S(1)}, bf16[8,8,2048]{2,1,0:T(8,128)(2,1)S(1)}, u32[]{:S(2)}, u32[]{:S(2)}) collective-permute-start(bf16[8,8,2048]{2,1,0:T(8,128)(2,1)S(1)} %broadcast_select_fusion.1), channel_id=1, source_target_pairs={{0,8},{4,12},{8,0},{12,4},{16,24},{20,28},{24,16},{28,20},{1,9},{5... | collective-permute-start | bytes 786440 | tf_op jit(solution)/shard_map/ppermute | solution.py:32
  16.4 5.7 %collective-permute-done.1 = bf16[8,8,2048]{2,1,0:T(8,128)(2,1)S(1)} collective-permute-done((bf16[8,8,2048]{2,1,0:T(8,128)(2,1)S(1)}, bf16[8,8,2048]{2,1,0:T(8,128)(2,1)S(1)}, u32[]{:S(2)}, u32[]{:S(2)}) %collective-permute-start.1) | collective-permute-done | bytes 262176 | tf_op jit(solution)/shard_map/ppermute | solution.py:32
  23.5 2.6 %collective-permute-start.2 = (bf16[8,8,2048]{2,1,0:T(8,128)(2,1)S(1)}, bf16[8,8,2048]{2,1,0:T(8,128)(2,1)S(1)}, u32[]{:S(2)}, u32[]{:S(2)}) collective-permute-start(bf16[8,8,2048]{2,1,0:T(8,128)(2,1)S(1)} %broadcast_select_fusion), channel_id=1, source_target_pairs={{0,16},{4,20},{8,24},{12,28},{16,0},{20,4},{24,8},{28,12},{1,17},{... | collective-permute-start | bytes 786440 | tf_op jit(solution)/shard_map/ppermute | solution.py:32
  26.1 10.6 %collective-permute-done.2 = bf16[8,8,2048]{2,1,0:T(8,128)(2,1)S(1)} collective-permute-done((bf16[8,8,2048]{2,1,0:T(8,128)(2,1)S(1)}, bf16[8,8,2048]{2,1,0:T(8,128)(2,1)S(1)}, u32[]{:S(2)}, u32[]{:S(2)}) %collective-permute-start.2) | collective-permute-done | bytes 262176 | tf_op jit(solution)/shard_map/ppermute | solution.py:32
  37.4 2.1 %fusion.34 = (f32[512]{0:T(512)S(1)}, f32[128,512]{1,0:T(8,128)S(1)}) fusion(bf16[2048,512]{1,0:T(8,128)(2,1)} %param.15, bf16[16,8,2048]{2,1,0:T(8,128)(2,1)S(1)} %scatter_fusion.2), kind=kOutput, calls=%fused_computation.111 | convolution fusion | flops 268500480 | bytes 2885632 | tf_op jit(solution)/shard_map/dot_general | solution.py:68
  39.5 5.7 %psum.42 = f32[512]{0:T(512)S(1)} all-reduce(f32[512]{0:T(512)S(1)} %get-tuple-element.34), channel_id=1, replica_groups=mesh['dp'=8,'bn'=4] {'bn'}, use_global_device_ids=true, to_apply=%region_8.10 | all-reduce | flops 512 | bytes 4096 | tf_op jit(solution)/shard_map/psum | solution.py:41
  45.2 6.5 %psum.43 = f32[512]{0:T(512)S(1)} all-reduce(f32[512]{0:T(512)S(1)} %multiply_reduce_fusion.2), channel_id=1, replica_groups=mesh['dp'=8,'bn'=4] {'bn'}, use_global_device_ids=true, to_apply=%region_10.12 | all-reduce | flops 512 | bytes 4096 | tf_op jit(solution)/shard_map/psum | solution.py:43
  51.9 1.8 %fusion.35 = (f32[512]{0:T(512)S(1)}, f32[128,512]{1,0:T(8,128)S(1)}) fusion(bf16[1536,512]{1,0:T(8,128)(2,1)} %bitcast.32, bf16[128,512]{1,0:T(8,128)(2,1)S(1)} %get-tuple-element.24, bf16[128,512]{1,0:T(8,128)(2,1)S(1)} %maximum_convert_fusion.2, bf16[128,512]{1,0:T(8,128)(2,1)S(1)} %get-tuple-element.23), kind=kOutput, calls=%fused_computation.112 | convolution fusion | flops 202571264 | bytes 2230272 | tf_op jit(solution)/shard_map/dot_general | solution.py:73
  53.7 5.7 %psum.44 = f32[512]{0:T(512)S(1)} all-reduce(f32[512]{0:T(512)S(1)} %get-tuple-element.36), channel_id=1, replica_groups=mesh['dp'=8,'bn'=4] {'bn'}, use_global_device_ids=true, to_apply=%region_12.14 | all-reduce | flops 512 | bytes 4096 | tf_op jit(solution)/shard_map/psum | solution.py:41
  59.4 6.2 %psum.45 = f32[512]{0:T(512)S(1)} all-reduce(f32[512]{0:T(512)S(1)} %multiply_reduce_fusion.1), channel_id=1, replica_groups=mesh['dp'=8,'bn'=4] {'bn'}, use_global_device_ids=true, to_apply=%region_14.16 | all-reduce | flops 512 | bytes 4096 | tf_op jit(solution)/shard_map/psum | solution.py:43
  65.7 1.4 fusion.36
  67.1 5.9 %psum.46 = f32[2048]{0:T(1024)S(1)} all-reduce(f32[2048]{0:T(1024)S(1)} %get-tuple-element.38), channel_id=1, replica_groups=mesh['dp'=8,'bn'=4] {'bn'}, use_global_device_ids=true, to_apply=%region_16.18 | all-reduce | flops 2048 | bytes 16384 | tf_op jit(solution)/shard_map/psum | solution.py:41
  73.0 1.4 multiply_reduce_fusion
  74.4 6.7 %psum.47 = f32[2048]{0:T(1024)S(1)} all-reduce(f32[2048]{0:T(1024)S(1)} %multiply_reduce_fusion), channel_id=1, replica_groups=mesh['dp'=8,'bn'=4] {'bn'}, use_global_device_ids=true, to_apply=%region_18.20 | all-reduce | flops 2048 | bytes 16384 | tf_op jit(solution)/shard_map/psum | solution.py:43
  81.1 1.7 %convert_reduce_fusion = f32[16,2048]{1,0:T(8,128)S(1)} fusion(bf16[16,8,2048]{2,1,0:T(8,128)(2,1)S(1)} %scatter_fusion.2, f32[2048]{0:T(1024)S(1)} %add_rsqrt_fusion.1, f32[128,2048]{1,0:T(8,128)} %get-tuple-element.39, f32[2048]{0:T(1024)S(1)} %broadcast_multiply_fusion), kind=kLoop, calls=%fused_computation.22 | loop fusion | flops 2064384 | bytes 1720320 | tf_op jit(solution)/shard_map/reduce_sum | solution.py:83
  84.5 2.7 %fusion.2 = f32[8192]{0:T(1024)S(1)} fusion(bf16[8192,128]{1,0:T(8,128)(2,1)} %param.20), kind=kLoop, calls=%fused_computation.18 | loop fusion | flops 3137536 | bytes 2129920 | tf_op jit(solution)/shard_map/reduce_sum | solution.py:37
  89.7 2.7 %collective-permute-done.4 = bf16[8,128]{1,0:T(8,128)(2,1)S(1)} collective-permute-done((bf16[8,128]{1,0:T(8,128)(2,1)S(1)}, bf16[8,128]{1,0:T(8,128)(2,1)S(1)}, u32[]{:S(2)}, u32[]{:S(2)}) %collective-permute-start.4) | collective-permute-done | bytes 2080 | tf_op jit(solution)/shard_map/ppermute | solution.py:32
  93.6 2.3 %collective-permute-start.5 = (bf16[8,128]{1,0:T(8,128)(2,1)S(1)}, bf16[8,128]{1,0:T(8,128)(2,1)S(1)}, u32[]{:S(2)}, u32[]{:S(2)}) collective-permute-start(bf16[8,128]{1,0:T(8,128)(2,1)S(1)} %broadcast_select_fusion.9), channel_id=1, source_target_pairs={{0,16},{4,20},{8,24},{12,28},{16,0},{20,4},{24,8},{28,12},{1,17},{... | collective-permute-start | bytes 6152 | tf_op jit(solution)/shard_map/ppermute | solution.py:32
  95.9 2.2 %collective-permute-done.5 = bf16[8,128]{1,0:T(8,128)(2,1)S(1)} collective-permute-done((bf16[8,128]{1,0:T(8,128)(2,1)S(1)}, bf16[8,128]{1,0:T(8,128)(2,1)S(1)}, u32[]{:S(2)}, u32[]{:S(2)}) %collective-permute-start.5) | collective-permute-done | bytes 2080 | tf_op jit(solution)/shard_map/ppermute | solution.py:32
  98.7 1.3 collective-permute-start.6
  100.1 2.3 %collective-permute-done.6 = bf16[1,16,128]{2,1,0:T(8,128)(2,1)S(1)} collective-permute-done((bf16[1,16,128]{2,1,0:T(8,128)(2,1)S(1)}, bf16[1,16,128]{2,1,0:T(8,128)(2,1)S(1)}, u32[]{:S(2)}, u32[]{:S(2)}) %collective-permute-start.6) | collective-permute-done | bytes 4128 | tf_op jit(solution)/shard_map/ppermute | solution.py:24
  102.4 1.4 collective-permute-start.7
  103.8 2.3 %collective-permute-done.7 = bf16[2,16,128]{2,1,0:T(8,128)(2,1)S(1)} collective-permute-done((bf16[2,16,128]{2,1,0:T(8,128)(2,1)S(1)}, bf16[2,16,128]{2,1,0:T(8,128)(2,1)S(1)}, u32[]{:S(2)}, u32[]{:S(2)}) %collective-permute-start.7) | collective-permute-done | bytes 8224 | tf_op jit(solution)/shard_map/ppermute | solution.py:24
  106.1 2.3 %collective-permute-start.8 = (bf16[4,16,128]{2,1,0:T(8,128)(2,1)S(1)}, bf16[4,16,128]{2,1,0:T(8,128)(2,1)S(1)}, u32[]{:S(2)}, u32[]{:S(2)}) collective-permute-start(bf16[4,16,128]{2,1,0:T(8,128)(2,1)S(1)} %pad_maximum_fusion.1), channel_id=1, source_target_pairs={{0,16},{4,20},{8,24},{12,28},{16,0},{20,4},{24,8},{28,12},{1,17},{... | collective-permute-start | bytes 49160 | tf_op jit(solution)/shard_map/ppermute | solution.py:24
  111.6 30.9 %all_gather.3 = bf16[128,128]{1,0:T(8,128)(2,1)S(1)} all-gather(bf16[16,128]{1,0:T(8,128)(2,1)S(1)} %get-tuple-element.14), channel_id=1, replica_groups=mesh['dp'=8,'bn'=4] {'dp'}, dimensions={0}, use_global_device_ids=true | all-gather | bytes 36864 | tf_op jit(solution)/shard_map/all_gather | solution.py:60
  142.5 3.4 %fusion.6 = f32[128]{0:T(128)S(1)} fusion(bf16[128,128]{1,0:T(8,128)(2,1)S(1)} %all_gather.3, bf16[8192,128]{1,0:T(8,128)(2,1)} %param.20, f32[8192]{0:T(1024)S(1)} %add_rsqrt_fusion), kind=kOutput, calls=%fused_computation.21 | convolution fusion | flops 274726784 | bytes 2163200 | tf_op jit(solution)/shard_map/dot_general | solution.py:94
  145.8 20.6 %all-reduce.1 = f32[128]{0:T(128)S(1)} all-reduce(f32[128]{0:T(128)S(1)} %fusion.6), channel_id=2, replica_groups=mesh['dp'=8,'bn'=4] {'dp'}, use_global_device_ids=true, to_apply=%region_27.30.clone | all-reduce | flops 128 | bytes 1024
  (72 shorter events, 15.5 us)
Async XLA Ops:
  0.0 65.7 %copy-start = (bf16[512,2048]{1,0:T(8,128)(2,1)S(1)}, bf16[512,2048]{1,0:T(8,128)(2,1)}, u32[]{:S(2)}) copy-start(bf16[512,2048]{1,0:T(8,128)(2,1)} %param.17) | copy-start | bytes 6291460
  3.8 9.3 %collective-permute-start = (bf16[8,8,2048]{2,1,0:T(8,128)(2,1)S(1)}, bf16[8,8,2048]{2,1,0:T(8,128)(2,1)S(1)}, u32[]{:S(2)}, u32[]{:S(2)}) collective-permute-start(bf16[8,8,2048]{2,1,0:T(8,128)(2,1)S(1)} %broadcast_select_fusion.2), channel_id=1, source_target_pairs={{0,4},{4,0},{8,12},{12,8},{16,20},{20,16},{24,28},{28,24},{1,5},{5... | collective-permute-start | bytes 786440 | tf_op jit(solution)/shard_map/ppermute | solution.py:32
  14.5 7.6 %collective-permute-start.1 = (bf16[8,8,2048]{2,1,0:T(8,128)(2,1)S(1)}, bf16[8,8,2048]{2,1,0:T(8,128)(2,1)S(1)}, u32[]{:S(2)}, u32[]{:S(2)}) collective-permute-start(bf16[8,8,2048]{2,1,0:T(8,128)(2,1)S(1)} %broadcast_select_fusion.1), channel_id=1, source_target_pairs={{0,8},{4,12},{8,0},{12,4},{16,24},{20,28},{24,16},{28,20},{1,9},{5... | collective-permute-start | bytes 786440 | tf_op jit(solution)/shard_map/ppermute | solution.py:32
  23.5 13.2 %collective-permute-start.2 = (bf16[8,8,2048]{2,1,0:T(8,128)(2,1)S(1)}, bf16[8,8,2048]{2,1,0:T(8,128)(2,1)S(1)}, u32[]{:S(2)}, u32[]{:S(2)}) collective-permute-start(bf16[8,8,2048]{2,1,0:T(8,128)(2,1)S(1)} %broadcast_select_fusion), channel_id=1, source_target_pairs={{0,16},{4,20},{8,24},{12,28},{16,0},{20,4},{24,8},{28,12},{1,17},{... | collective-permute-start | bytes 786440 | tf_op jit(solution)/shard_map/ppermute | solution.py:32
  67.1 15.7 %copy-start.1 = (bf16[2048,128]{1,0:T(8,128)(2,1)S(1)}, bf16[2048,128]{1,0:T(8,128)(2,1)}, u32[]{:S(2)}) copy-start(bf16[2048,128]{1,0:T(8,128)(2,1)} %param.18) | copy-start | bytes 1572868
  81.1 14.8 %copy-start.3 = (s32[16]{0:T(128)S(1)}, s32[16]{0:T(128)}, u32[]{:S(2)}) copy-start(s32[16]{0:T(128)} %param.21) | copy-start | bytes 196
  81.1 18.8 %copy-start.2 = (bf16[16,128]{1,0:T(8,128)(2,1)S(1)}, bf16[16,128]{1,0:T(8,128)(2,1)}, u32[]{:S(2)}) copy-start(bf16[16,128]{1,0:T(8,128)(2,1)} %param.19) | copy-start | bytes 12292
  81.1 27.3 %copy-start.4 = (u32[32]{0:T(128)S(1)}, u32[32]{0:T(128)}, u32[]{:S(2)}) copy-start(u32[32]{0:T(128)} %constant.129) | copy-start | bytes 388
  83.9 3.6 %collective-permute-start.3 = (bf16[8,128]{1,0:T(8,128)(2,1)S(1)}, bf16[8,128]{1,0:T(8,128)(2,1)S(1)}, u32[]{:S(2)}, u32[]{:S(2)}) collective-permute-start(bf16[8,128]{1,0:T(8,128)(2,1)S(1)} %broadcast_select_fusion.11), channel_id=1, source_target_pairs={{0,4},{4,0},{8,12},{12,8},{16,20},{20,16},{24,28},{28,24},{1,5},{5... | collective-permute-start | bytes 6152 | tf_op jit(solution)/shard_map/ppermute | solution.py:32
  88.8 3.6 %collective-permute-start.4 = (bf16[8,128]{1,0:T(8,128)(2,1)S(1)}, bf16[8,128]{1,0:T(8,128)(2,1)S(1)}, u32[]{:S(2)}, u32[]{:S(2)}) collective-permute-start(bf16[8,128]{1,0:T(8,128)(2,1)S(1)} %broadcast_select_fusion.10), channel_id=1, source_target_pairs={{0,8},{4,12},{8,0},{12,4},{16,24},{20,28},{24,16},{28,20},{1,9},{5... | collective-permute-start | bytes 6152 | tf_op jit(solution)/shard_map/ppermute | solution.py:32
  93.6 4.5 %collective-permute-start.5 = (bf16[8,128]{1,0:T(8,128)(2,1)S(1)}, bf16[8,128]{1,0:T(8,128)(2,1)S(1)}, u32[]{:S(2)}, u32[]{:S(2)}) collective-permute-start(bf16[8,128]{1,0:T(8,128)(2,1)S(1)} %broadcast_select_fusion.9), channel_id=1, source_target_pairs={{0,16},{4,20},{8,24},{12,28},{16,0},{20,4},{24,8},{28,12},{1,17},{... | collective-permute-start | bytes 6152 | tf_op jit(solution)/shard_map/ppermute | solution.py:32
  98.7 3.7 %collective-permute-start.6 = (bf16[1,16,128]{2,1,0:T(8,128)(2,1)S(1)}, bf16[1,16,128]{2,1,0:T(8,128)(2,1)S(1)}, u32[]{:S(2)}, u32[]{:S(2)}) collective-permute-start(bf16[1,16,128]{2,1,0:T(8,128)(2,1)S(1)} %bitcast.30), channel_id=1, source_target_pairs={{0,4},{4,0},{8,12},{12,8},{16,20},{20,16},{24,28},{28,24},{1,5},{5... | collective-permute-start | bytes 12296 | tf_op jit(solution)/shard_map/ppermute | solution.py:24
  102.4 3.7 %collective-permute-start.7 = (bf16[2,16,128]{2,1,0:T(8,128)(2,1)S(1)}, bf16[2,16,128]{2,1,0:T(8,128)(2,1)S(1)}, u32[]{:S(2)}, u32[]{:S(2)}) collective-permute-start(bf16[2,16,128]{2,1,0:T(8,128)(2,1)S(1)} %pad_maximum_fusion.2), channel_id=1, source_target_pairs={{0,8},{4,12},{8,0},{12,4},{16,24},{20,28},{24,16},{28,20},{1,9},{5... | collective-permute-start | bytes 24584 | tf_op jit(solution)/shard_map/ppermute | solution.py:24
  106.1 4.7 %collective-permute-start.8 = (bf16[4,16,128]{2,1,0:T(8,128)(2,1)S(1)}, bf16[4,16,128]{2,1,0:T(8,128)(2,1)S(1)}, u32[]{:S(2)}, u32[]{:S(2)}) collective-permute-start(bf16[4,16,128]{2,1,0:T(8,128)(2,1)S(1)} %pad_maximum_fusion.1), channel_id=1, source_target_pairs={{0,16},{4,20},{8,24},{12,28},{16,0},{20,4},{24,8},{28,12},{1,17},{... | collective-permute-start | bytes 49160 | tf_op jit(solution)/shard_map/ppermute | solution.py:24
